TPU v7x, 32 devices: a whole 2x2x4 slice. The times are simulated.
32 devices in a mesh: slab: 8 (over z, core), loop: 4 (over y, x).
Axes of the slice: x: 2, y: 2, z: 4, core: 2. Of those that a mesh axis runs over, the one named last changes fastest.
Arguments:
- doc_pool: bfloat16 [8, 4, 256, 4096], P('slab', 'loop'), may hold values from -6 to 6
- cand_owner: int32 [8, 4, 16, 1], P('slab', 'loop'), may hold values from 0 to 7; in each aligned block of 16 rows (0 to 15, 16 to 31, ..., all dimensions but the last counted through in order) at most 4 rows name the same one
- cand_row: int32 [8, 4, 16], P('slab', 'loop'), may hold values from 0 to 255
- elements: bfloat16 [8, 4, 2048, 4096], P('slab', 'loop'), may hold values from -6 to 6
- coverage: float32 [8, 4, 2048], P('slab', 'loop'), may hold values from -0.5 to 1.5
- elem_weight: float32 [8, 4, 2048], P('slab', 'loop'), may hold values from 1 to 10
Outputs:
- gains: float32 [8, 4, 16], P('slab', 'loop')
Inputs may be any that keep to these rules, and one draw needn't show every extreme that they name: `cand_owner`: among the candidates of one device, at most 4 name the same owner; some owner is named exactly 4 times.
All inputs are finite; a program needn't handle non-finite values.
Results may differ from a plain program's by a relative error of at most 0.0003.
Values may be sent and summed in bfloat16 or wider, within the bound.
A program may use at most 128 MiB of HBM per device.

v0:
```python
import functools

import jax
import jax.numpy as jnp
from jax import lax
from jax.experimental import pallas as pl
from jax.experimental.pallas import tpu as pltpu
from jax.sharding import PartitionSpec as P

MESH = pl.DeviceIdType.MESH
LANES = 128
SUB = 8


def kernel(
    dims,
    owner_ref, row_ref, cover_ref, weight_ref, pool_hbm, docs_hbm,
    out_ref,
    pool, docs, req_out, req_in, picked, fetched, cand, acc, part, slab_terms,
    loop_terms,
    pool_sem, docs_sem, req_send, req_recv, pick_send, pick_recv, self_sem,
    unit_send, line_send, unit_recv, slab_send, slab_recv, loop_send, loop_recv,
):
    slabs, loops, share, cap, chunks, chunk, tile, total_docs, scale = dims
    lines = slabs // 2
    units = slabs * loops
    rows_pool = pool.shape[0]
    n_docs = docs.shape[1]
    slab = lax.axis_index("slab")
    loop = lax.axis_index("loop")
    line = slab // 2
    core = lax.rem(slab, 2)
    me = slab * loops + loop
    half = loops // 2
    pieces = 4

    def loop_of(pos):
        return jnp.where(pos < half, 2 * pos, 2 * (loops - 1 - pos) + 1)

    here = jnp.where(lax.rem(loop, 2) == 0, loop // 2, loops - 1 - loop // 2)
    ahead = loop_of(lax.rem(here + 1, loops))
    behind = loop_of(lax.rem(here + loops - 1, loops))

    pool_copy = [
        pltpu.make_async_copy(
            pool_hbm.at[:, pl.ds(k * chunk, chunk)],
            pool.at[:, pl.ds(k * chunk, chunk)],
            pool_sem.at[k],
        )
        for k in range(chunks)
    ]
    docs_copy = [
        pltpu.make_async_copy(
            docs_hbm.at[:, pl.ds(k * chunk, chunk)], docs.at[k], docs_sem.at[k]
        )
        for k in range(chunks)
    ]

    barrier = pltpu.get_barrier_semaphore()

    def greet(device):
        pl.semaphore_signal(barrier, inc=1, device_id=device, device_id_type=MESH)

    for d in range(1, slabs):
        greet((lax.rem(slab + d, slabs), loop))
    for d in range(1, loops):
        greet((slab, lax.rem(loop + d, loops)))
    for k in range(chunks):
        pool_copy[k].start()
    for k in range(chunks):
        docs_copy[k].start()

    owner_row = owner_ref[...]
    row_row = row_ref[...]
    down = lax.broadcasted_iota(jnp.int32, (share, share), 0)
    across = lax.broadcasted_iota(jnp.int32, (share, share), 1)
    wide = jnp.broadcast_to(owner_row, (share, share)).astype(jnp.float32)
    owner_col = jnp.sum(jnp.where(down == across, wide, 0.0), axis=1, keepdims=True)
    rank_row = jnp.sum(
        jnp.where((owner_col == wide) & (down < across), 1.0, 0.0), axis=0, keepdims=True
    )
    owner_f = owner_row.astype(jnp.float32)
    asked_row = owner_f * SUB + rank_row
    slot_row = owner_f * cap + rank_row
    slot_col = jnp.sum(
        jnp.where(down == across, jnp.broadcast_to(slot_row, (share, share)), 0.0),
        axis=1, keepdims=True,
    )
    place = lax.broadcasted_iota(jnp.int32, (slabs * SUB, share), 0).astype(jnp.float32)
    asked = jnp.sum(
        jnp.where(place == asked_row, row_row.astype(jnp.float32), 0.0), axis=1, keepdims=True
    )
    req_out[...] = jnp.broadcast_to(asked, (slabs * SUB, LANES)).astype(jnp.int32).reshape(
        slabs, SUB, LANES
    )
    choose = jnp.where(
        slot_col == lax.broadcasted_iota(jnp.int32, (share, slabs * cap), 1).astype(jnp.float32),
        1.0, 0.0,
    ).astype(jnp.bfloat16)

    pl.semaphore_wait(barrier, slabs + loops - 2)

    def req_copy(d):
        other = lax.rem(slab + d, slabs)
        return pltpu.make_async_remote_copy(
            src_ref=req_out.at[other], dst_ref=req_in.at[slab],
            send_sem=req_send.at[d], recv_sem=req_recv.at[d],
            device_id=(other, loop), device_id_type=MESH,
        )

    for d in range(1, slabs):
        req_copy(d).start()
    own_req = pltpu.make_async_copy(req_out.at[slab], req_in.at[slab], self_sem.at[chunks])
    own_req.start()
    own_req.wait()
    for d in range(1, slabs):
        req_copy(d).wait()

    wanted = req_in[...].reshape(slabs * SUB, LANES)
    lane = lax.broadcasted_iota(jnp.int32, (slabs * SUB, LANES), 1)
    pick = jnp.concatenate(
        [
            jnp.where(wanted == lane + b * LANES, 1.0, 0.0).astype(jnp.bfloat16)
            for b in range(rows_pool // LANES)
        ],
        axis=1,
    )

    def pick_copy(k, d):
        other = lax.rem(slab + d, slabs)
        return pltpu.make_async_remote_copy(
            src_ref=picked.at[k, other], dst_ref=fetched.at[k, slab],
            send_sem=pick_send.at[k, d], recv_sem=pick_recv.at[k, d],
            device_id=(other, loop), device_id_type=MESH,
        )

    def own_pick(k):
        return pltpu.make_async_copy(picked.at[k, slab], fetched.at[k, slab], self_sem.at[k])

    def gather(k):
        pool_copy[k].wait()
        rows = jnp.dot(
            pick, pool[:, k * chunk:(k + 1) * chunk], preferred_element_type=jnp.float32
        )
        for r in range(slabs):
            picked[k, r] = rows[r * SUB:r * SUB + cap].astype(jnp.bfloat16)
        for d in range(1, slabs):
            pick_copy(k, d).start()
        own_pick(k).start()

    def unit_of(j, pos, c):
        return (2 * j + c) * loops + loop_of(pos)

    def unit_copy(k, j, pos, way):
        u = unit_of(j, pos, core)
        device = ((slab, ahead), (slab, behind), (2 * line + 1 - core, loop))[way]
        return pltpu.make_async_remote_copy(
            src_ref=cand.at[k, u], dst_ref=cand.at[k, u],
            send_sem=unit_send.at[k, j * loops + pos, way], recv_sem=unit_recv.at[k, u],
            device_id=device, device_id_type=MESH,
        )

    def line_copy(k, d):
        return pltpu.make_async_remote_copy(
            src_ref=cand.at[k, me], dst_ref=cand.at[k, me],
            send_sem=line_send.at[k, d], recv_sem=unit_recv.at[k, me],
            device_id=(lax.rem(slab + 2 * d, slabs), loop), device_id_type=MESH,
        )

    def arrive(k, j, pos, c):
        u = unit_of(j, pos, c)
        pltpu.make_async_remote_copy(
            src_ref=cand.at[k, u], dst_ref=cand.at[k, u],
            send_sem=unit_send.at[k, 0, 0], recv_sem=unit_recv.at[k, u],
            device_id=(2 * line + 1 - core, loop), device_id_type=MESH,
        ).wait_recv()

    reach_even, reach_odd = half, loops - 1 - half

    def forward(k, j, pos, finish=False):
        def act(cond, way):
            @pl.when(cond)
            def _():
                copy = unit_copy(k, j, pos, way)
                if finish:
                    copy.wait_send()
                else:
                    copy.start()
        from_here = pos == here
        far_ahead = lax.rem(here - pos + loops, loops)
        far_behind = lax.rem(pos - here + loops, loops)
        reach_ahead = jnp.where(core == 0, reach_even, reach_odd)
        reach_behind = jnp.where(core == 0, reach_odd, reach_even)
        by_ahead = far_ahead <= reach_ahead
        act(from_here | (by_ahead & (far_ahead < reach_ahead)), 0)
        act(from_here | (jnp.logical_not(by_ahead) & (far_behind < reach_behind)), 1)
        act(from_here | True, 2)

    def nearby(first, action):
        def step(t, _):
            far = (t + 1) // 2
            j = jnp.where(lax.rem(t, 2) == 1, line - far, line + far)

            @pl.when((j >= 0) & (j < lines))
            def _():
                action(j)
            return 0
        lax.fori_loop(first, 2 * lines - 1, step, 0)

    def own(k):
        own_pick(k).wait()
        for d in range(1, slabs):
            pick_copy(k, d).wait()
        rows = jnp.concatenate(
            [fetched[k, o].astype(jnp.float32) for o in range(slabs)], axis=0
        ).astype(jnp.bfloat16)
        mine = jnp.dot(choose, rows, preferred_element_type=jnp.float32)
        cand[k, me] = mine.astype(jnp.bfloat16)
        forward(k, line, here)
        for d in range(1, lines):
            line_copy(k, d).start()

    def column(k):
        def action(j):
            arrive(k, j, here, core)
            forward(k, j, here)
        nearby(1, action)

    def ring(k, e):
        def action(j):
            behind_pos = lax.rem(here - e + loops, loops)
            ahead_pos = lax.rem(here + e, loops)
            reach_ahead = jnp.where(core == 0, reach_even, reach_odd)
            reach_behind = jnp.where(core == 0, reach_odd, reach_even)

            @pl.when(e <= reach_ahead)
            def _():
                arrive(k, j, behind_pos, core)
                forward(k, j, behind_pos)

            @pl.when(e <= reach_behind)
            def _():
                arrive(k, j, ahead_pos, core)
                forward(k, j, ahead_pos)
        nearby(0, action)

    def sibling(k):
        def step(t, _):
            arrive(k, t // loops, lax.rem(t, loops), 1 - core)
            return 0
        lax.fori_loop(0, lines * loops, step, 0)

    def multiply(k, piece):
        if piece == 0:
            docs_copy[k].wait()
        share_all = cand[k].reshape(units * share, chunk)
        rows = n_docs // pieces
        for i in range(rows // tile):
            at = pl.ds(piece * rows + i * tile, tile)
            product = lax.dot_general(
                docs[k, at, :], share_all, (((1,), (1,)), ((), ())),
                preferred_element_type=jnp.float32,
            )
            if k == 0:
                acc[at, :] = product
            else:
                acc[at, :] += product

    for k in range(chunks):
        gather(k)
    for k in range(min(2, chunks)):
        own(k)
    for t in range(chunks + half + 1):
        stages = []
        if 0 < t < chunks - 1:
            stages.append(functools.partial(own, t + 1))
        if t < chunks:
            stages.append(functools.partial(column, t))
        for e in range(1, half + 1):
            if 0 <= t - e < chunks:
                stages.append(functools.partial(ring, t - e, e))
        if 0 <= t - half < chunks:
            stages.append(functools.partial(sibling, t - half))
        done = t - half - 1
        for piece in range(max(pieces, len(stages))):
            if piece < len(stages):
                stages[piece]()
            if done >= 0 and piece < pieces:
                multiply(done, piece)

    cover_cols = jnp.transpose(cover_ref[...])
    weight_cols = jnp.transpose(weight_ref[...])
    total = jnp.zeros((1, units * share), jnp.float32)
    for j in range(n_docs // LANES):
        s = acc[j * LANES:(j + 1) * LANES, :] * scale
        gain = weight_cols[:, j:j + 1] * jnp.maximum(s - cover_cols[:, j:j + 1], 0.0)
        total = total + jnp.sum(gain, axis=0, keepdims=True)
    total = total / total_docs
    for r in range(units * share // LANES):
        part[r] = total[:, r * LANES:(r + 1) * LANES]
    per_row = LANES // (loops * share)

    def slab_term(d):
        other = lax.rem(slab + d, slabs)
        return pltpu.make_async_remote_copy(
            src_ref=part.at[other // per_row], dst_ref=slab_terms.at[d],
            send_sem=slab_send.at[d], recv_sem=slab_recv.at[d],
            device_id=(other, loop), device_id_type=MESH,
        )

    def loop_term(d):
        return pltpu.make_async_remote_copy(
            src_ref=loop_terms.at[0], dst_ref=loop_terms.at[d],
            send_sem=loop_send.at[d], recv_sem=loop_recv.at[d],
            device_id=(slab, lax.rem(loop + d, loops)), device_id_type=MESH,
        )

    for d in range(1, slabs):
        slab_term(d).start()
    slab_terms[0] = part[slab // per_row]
    for k in range(chunks):
        for d in range(1, lines):
            line_copy(k, d).wait_send()

        def finish(t, _, k=k):
            forward(k, t // loops, lax.rem(t, loops), finish=True)
            return 0
        lax.fori_loop(0, lines * loops, finish, 0)
    for d in range(1, slabs):
        slab_term(d).wait()
    loop_terms[0] = jnp.sum(slab_terms[...], axis=0)
    for d in range(1, loops):
        loop_term(d).start()
    for d in range(1, loops):
        loop_term(d).wait()
    row = jnp.sum(loop_terms[...], axis=0)
    first = lax.rem(slab, per_row) * loops * share + loop * share
    mine = lax.broadcasted_iota(jnp.int32, (LANES, LANES), 0)
    to = lax.broadcasted_iota(jnp.int32, (LANES, LANES), 1)
    column_of = jnp.sum(
        jnp.where(mine == to, jnp.broadcast_to(row, (LANES, LANES)), 0.0), axis=1, keepdims=True
    )
    moved = jnp.sum(jnp.where(mine == to + first, column_of, 0.0), axis=0, keepdims=True)
    out_ref[...] = moved[:, :share]


def body(dims, doc_pool, cand_owner, cand_row, elements, coverage, elem_weight):
    slabs, loops, share, cap, chunks, chunk, tile, _, _ = dims
    pool_rows, width = doc_pool.shape[2:]
    n_docs = elements.shape[2]
    units = slabs * loops
    vmem = pl.BlockSpec(memory_space=pltpu.VMEM)
    hbm = pl.BlockSpec(memory_space=pl.ANY)
    dma = pltpu.SemaphoreType.DMA
    out = pl.pallas_call(
        functools.partial(kernel, dims),
        out_shape=jax.ShapeDtypeStruct((1, share), jnp.float32),
        in_specs=[vmem, vmem, vmem, vmem, hbm, hbm],
        out_specs=vmem,
        scratch_shapes=[
            pltpu.VMEM((pool_rows, width), jnp.bfloat16),
            pltpu.VMEM((chunks, n_docs, chunk), jnp.bfloat16),
            pltpu.VMEM((slabs, SUB, LANES), jnp.int32),
            pltpu.VMEM((slabs, SUB, LANES), jnp.int32),
            pltpu.VMEM((chunks, slabs, cap, chunk), jnp.bfloat16),
            pltpu.VMEM((chunks, slabs, cap, chunk), jnp.bfloat16),
            pltpu.VMEM((chunks, units, share, chunk), jnp.bfloat16),
            pltpu.VMEM((n_docs, units * share), jnp.float32),
            pltpu.VMEM((units * share // LANES, 1, LANES), jnp.float32),
            pltpu.VMEM((slabs, 1, LANES), jnp.float32),
            pltpu.VMEM((loops, 1, LANES), jnp.float32),
            dma((chunks,)),
            dma((chunks,)),
            dma((slabs,)),
            dma((slabs,)),
            dma((chunks, slabs)),
            dma((chunks, slabs)),
            dma((chunks + 1,)),
            dma((chunks, units // 2, 3)),
            dma((chunks, slabs // 2)),
            dma((chunks, units)),
            dma((slabs,)),
            dma((slabs,)),
            dma((loops,)),
            dma((loops,)),
        ],
        compiler_params=pltpu.CompilerParams(
            collective_id=0, has_side_effects=True, vmem_limit_bytes=60 * 2**20
        ),
    )(
        cand_owner.reshape(1, share),
        cand_row.reshape(1, share),
        coverage.reshape(n_docs // LANES, LANES),
        elem_weight.reshape(n_docs // LANES, LANES),
        doc_pool.reshape(pool_rows, width),
        elements.reshape(n_docs, width),
    )
    return out.reshape(1, 1, share)


def solution(mesh):
    slabs, loops = mesh.shape["slab"], mesh.shape["loop"]

    def whole(doc_pool, cand_owner, cand_row, elements, coverage, elem_weight):
        share = cand_row.shape[2]
        width = doc_pool.shape[3]
        n_docs = elements.shape[2]
        cap = max(2, 2 * share // slabs)
        chunks = 4
        dims = (
            slabs, loops, share, cap, chunks, width // chunks, min(512, n_docs),
            float(n_docs * slabs * loops), float(width) ** (-0.5),
        )
        placed = (
            P("slab", "loop", None, None),
            P("slab", "loop", None, None),
            P("slab", "loop", None),
            P("slab", "loop", None, None),
            P("slab", "loop", None),
            P("slab", "loop", None),
        )
        return jax.shard_map(
            functools.partial(body, dims), mesh=mesh, in_specs=placed,
            out_specs=P("slab", "loop", None), check_vma=False,
        )(doc_pool, cand_owner, cand_row, elements, coverage, elem_weight)

    return whole
```

profile of v0, /device:TPU:0, one launch (start us, length us, event | category | flops | bytes accessed | tf_op | source)
XLA Modules:
  0.0 58.2 jit_solution(9577699340063717886)
XLA Ops:
  0.0 57.0 %shard_map.64 = f32[1,16]{1,0:T(1,128)} custom-call(s32[1,16]{1,0:T(1,128)} %bitcast.11, s32[1,16]{1,0:T(1,128)} %bitcast.12, f32[16,128]{1,0:T(8,128)} %bitcast.9, f32[16,128]{1,0:T(8,128)} %bitcast.10, bf16[256,4096]{1,0:T(8,128)(2,1)} %bitcast.8, bf16[2048,4096]{1,0:T(8,128)(2,1)} %bitcast.7), custom_call_target="tpu_custom_call" | custom-call | tf_op jit(solution)/shard_map/pallas_call | solution.py:355
  57.0 1.2 %copy.8 = f32[1,1,16]{2,1,0:T(1,128)} copy(f32[1,1,16]{2,1,0:T(1,128)} %bitcast.13) | data formatting | bytes 128
where the time goes:
time: 58.4 us; the launch traced here: 58.2 us
  Pallas kernels  57 us (98%)
  local copies, waits for them, and re-layouts  1.19 us (2%)
    pallas_call x1, Pallas kernels, body(): pl.pallas_call(functools.partial(kernel, dims), out_shape=jax.ShapeDtypeS...  57 us
    unnamed x1, local copies, waits for them, and re-layouts  1.19 us

commit v1 on v0

v1 whole, which is shorter than its diff:
```python
import functools

import jax
import jax.numpy as jnp
from jax import lax
from jax.experimental import pallas as pl
from jax.experimental.pallas import tpu as pltpu
from jax.sharding import PartitionSpec as P

MESH = pl.DeviceIdType.MESH
LANES = 128
SUB = 8
CHUNKS = 8
RING_LAG = 2
HOP_LAG = 2
LAST_LAG = 1


def kernel(
    dims,
    owner_ref, row_ref, cover_ref, weight_ref, pool_hbm, docs_hbm,
    out_ref,
    pool, docs, req_out, req_in, picked, fetched, cand, acc, part, terms,
    pool_sem, docs_sem, req_send, req_recv, pick_send, pick_recv,
    cand_send, relay_send, line_recv, ring_recv, pair_recv, term_send, term_recv,
):
    slabs, loops, share, cap, chunks, chunk, tile, total_docs, scale = dims
    lines = slabs // 2
    units = slabs * loops
    rows_pool = pool.shape[0]
    n_docs = docs.shape[0]
    slab = lax.axis_index("slab")
    loop = lax.axis_index("loop")
    line = slab // 2
    core = lax.rem(slab, 2)
    me = slab * loops + loop
    half = loops // 2
    reach_even, reach_odd = half, loops - 1 - half
    relayed = lines == 4

    def loop_of(pos):
        return jnp.where(pos < half, 2 * pos, 2 * (loops - 1 - pos) + 1)

    def pos_of(at):
        return jnp.where(lax.rem(at, 2) == 0, at // 2, loops - 1 - at // 2)

    here = pos_of(loop)
    ahead = loop_of(lax.rem(here + 1, loops))
    behind = loop_of(lax.rem(here + loops - 1, loops))

    pool_copy = pltpu.make_async_copy(pool_hbm, pool, pool_sem.at[0])
    docs_copy = pltpu.make_async_copy(docs_hbm, docs, docs_sem.at[0])

    barrier = pltpu.get_barrier_semaphore()

    def greet(device):
        pl.semaphore_signal(barrier, inc=1, device_id=device, device_id_type=MESH)

    for d in range(1, slabs):
        greet((lax.rem(slab + d, slabs), loop))
    for d in range(1, loops):
        greet((slab, lax.rem(loop + d, loops)))
    pool_copy.start()
    docs_copy.start()

    owner_row = owner_ref[...]
    row_row = row_ref[...]
    down = lax.broadcasted_iota(jnp.int32, (share, share), 0)
    across = lax.broadcasted_iota(jnp.int32, (share, share), 1)
    wide = jnp.broadcast_to(owner_row, (share, share)).astype(jnp.float32)
    owner_col = jnp.sum(jnp.where(down == across, wide, 0.0), axis=1, keepdims=True)
    rank_row = jnp.sum(
        jnp.where((owner_col == wide) & (down < across), 1.0, 0.0), axis=0, keepdims=True
    )
    owner_f = owner_row.astype(jnp.float32)
    asked_row = owner_f * SUB + rank_row
    slot_row = owner_f * cap + rank_row
    slot_col = jnp.sum(
        jnp.where(down == across, jnp.broadcast_to(slot_row, (share, share)), 0.0),
        axis=1, keepdims=True,
    )
    place = lax.broadcasted_iota(jnp.int32, (slabs * SUB, share), 0).astype(jnp.float32)
    asked = jnp.sum(
        jnp.where(place == asked_row, row_row.astype(jnp.float32), 0.0), axis=1, keepdims=True
    )
    req_out[...] = jnp.broadcast_to(asked, (slabs * SUB, LANES)).astype(jnp.int32).reshape(
        slabs, SUB, LANES
    )
    choose = jnp.where(
        slot_col == lax.broadcasted_iota(jnp.int32, (share, slabs * cap), 1).astype(jnp.float32),
        1.0, 0.0,
    ).astype(jnp.bfloat16)

    pl.semaphore_wait(barrier, slabs + loops - 2)

    def remote(src, dst, send, recv, device):
        return pltpu.make_async_remote_copy(
            src_ref=src, dst_ref=dst, send_sem=send, recv_sem=recv,
            device_id=device, device_id_type=MESH,
        )

    def settle(ref, sem):
        pltpu.make_async_copy(ref, ref, sem).wait()

    for d in range(1, slabs):
        other = lax.rem(slab + d, slabs)
        remote(
            req_out.at[other], req_in.at[slab], req_send.at[0], req_recv.at[0], (other, loop)
        ).start()
    req_in[slab] = req_out[slab]
    pool_copy.wait()
    settle(req_in.at[pl.ds(0, slabs - 1)], req_recv.at[0])

    wanted = req_in[...].reshape(slabs * SUB, LANES)
    lane = lax.broadcasted_iota(jnp.int32, (slabs * SUB, LANES), 1)
    pick = jnp.concatenate(
        [
            jnp.where(wanted == lane + b * LANES, 1.0, 0.0).astype(jnp.bfloat16)
            for b in range(rows_pool // LANES)
        ],
        axis=1,
    )

    def gather(k):
        rows = jnp.dot(
            pick, pool[:, k * chunk:(k + 1) * chunk], preferred_element_type=jnp.float32
        )
        for r in range(slabs):
            picked[k, r] = rows[r * SUB:r * SUB + cap].astype(jnp.bfloat16)
        for d in range(1, slabs):
            other = lax.rem(slab + d, slabs)
            remote(
                picked.at[k, other], fetched.at[k, slab], pick_send.at[0], pick_recv.at[k],
                (other, loop),
            ).start()
        fetched[k, slab] = picked[k, slab]

    def to_ring(k, block, e, way):
        slot = e - 1 if way == 0 else jnp.where(core == 0, reach_even, reach_odd) + e - 1
        remote(
            block, block, cand_send.at[0], ring_recv.at[k, slot],
            (slab, ahead if way == 0 else behind),
        ).start()

    def to_pair(k, pos):
        block = cand.at[k, core, pos]
        remote(
            block, block, cand_send.at[0], pair_recv.at[k], (2 * line + 1 - core, loop)
        ).start()

    edge = (line == 0) | (line == lines - 1)

    def own(k):
        settle(fetched.at[k, pl.ds(0, slabs - 1)], pick_recv.at[k])
        rows = jnp.concatenate(
            [fetched[k, o].astype(jnp.float32) for o in range(slabs)], axis=0
        ).astype(jnp.bfloat16)
        mine = jnp.dot(choose, rows, preferred_element_type=jnp.float32)
        cand[k, core, here, line] = mine.astype(jnp.bfloat16)
        block = cand.at[k, core, here, line]
        if relayed:
            targets = [
                jnp.where(edge, jnp.where(line == 0, 2, 1), lines - 1 - line),
                jnp.where(edge, jnp.where(line == 0, 1, 2), jnp.where(line == 1, 0, 3)),
            ]
        else:
            targets = [lax.rem(line + d, lines) for d in range(1, lines)]
        for to in targets:
            remote(
                block, block, cand_send.at[0], line_recv.at[k], (2 * to + core, loop)
            ).start()
        to_ring(k, block, 1, 0)
        to_ring(k, block, 1, 1)

    def column(k):
        settle(cand.at[k, 0, 0, pl.ds(0, lines - 1)], line_recv.at[k])
        if relayed:
            @pl.when(jnp.logical_not(edge))
            def _():
                block = cand.at[k, core, here, pl.ds(jnp.where(line == 1, 2, 0), 2)]
                remote(
                    block, block, relay_send.at[0], line_recv.at[k],
                    (2 * jnp.where(line == 1, 0, 3) + core, loop),
                ).start()
        for d in range(1, lines):
            block = cand.at[k, core, here, lax.rem(line + d, lines)]
            to_ring(k, block, 1, 0)
            to_ring(k, block, 1, 1)
        to_pair(k, here)

    def ring(k, e):
        for way in (0, 1):
            reach = (reach_even, reach_odd) if way == 0 else (reach_odd, reach_even)
            limit = jnp.where(core == 0, reach[0], reach[1])
            pos = lax.rem(here - e + loops if way == 0 else here + e, loops)
            block = cand.at[k, core, pos]

            def arrive(way=way, reach=reach, limit=limit, pos=pos, block=block):
                slot = e - 1 if way == 0 else jnp.where(core == 0, reach_even, reach_odd) + e - 1
                settle(block, ring_recv.at[k, slot])
                if e < min(reach):
                    to_ring(k, block, e + 1, way)
                elif e < max(reach):
                    @pl.when(e < limit)
                    def _():
                        to_ring(k, block, e + 1, way)
                to_pair(k, pos)

            if e <= min(reach):
                arrive()
            elif e <= max(reach):
                pl.when(e <= limit)(arrive)

    cover_cols = jnp.transpose(cover_ref[...])
    weight_cols = jnp.transpose(weight_ref[...])
    tiles = n_docs // tile

    def multiply(k, i):
        if k == 0 and i == 0:
            docs_copy.wait()
        share_all = cand[k].reshape(units * share, chunk)
        at = slice(i * tile, (i + 1) * tile)
        product = lax.dot_general(
            docs[at, k * chunk:(k + 1) * chunk], share_all, (((1,), (1,)), ((), ())),
            preferred_element_type=jnp.float32,
        )
        if k == 0:
            acc[at, :] = product
        elif k < chunks - 1:
            acc[at, :] += product
        else:
            scores = (acc[at, :] + product) * scale
            total = jnp.zeros((1, units * share), jnp.float32)
            for j in range(tile // LANES):
                col = i * (tile // LANES) + j
                s = scores[j * LANES:(j + 1) * LANES, :]
                gain = weight_cols[:, col:col + 1] * jnp.maximum(
                    s - cover_cols[:, col:col + 1], 0.0
                )
                total = total + jnp.sum(gain, axis=0, keepdims=True)
            return total

    for k in range(chunks):
        gather(k)
    for k in range(chunks):
        own(k)
    lags = [RING_LAG + HOP_LAG * (e - 1) for e in range(1, half + 1)]
    final = lags[-1] + LAST_LAG
    total = jnp.zeros((1, units * share), jnp.float32)
    for t in range(chunks + final):
        stages = []
        if t < chunks:
            stages.append(functools.partial(column, t))
        for e in range(1, half + 1):
            if 0 <= t - lags[e - 1] < chunks:
                stages.append(functools.partial(ring, t - lags[e - 1], e))
        done = t - final
        if done >= 0:
            settle(cand.at[done, 0], pair_recv.at[done])
        for n in range(max(tiles, len(stages))):
            if n < len(stages):
                stages[n]()
            if done >= 0 and n < tiles:
                gains = multiply(done, n)
                if gains is not None:
                    total = total + gains
    total = total / total_docs
    for r in range(units * share // LANES):
        part[r] = total[:, r * LANES:(r + 1) * LANES]

    def first_of(s, p):
        return ((lax.rem(s, 2) * loops + pos_of(p)) * lines + s // 2) * share

    for d in range(slabs):
        for e in range(loops):
            if d + e > 0:
                s, p = lax.rem(slab + d, slabs), lax.rem(loop + e, loops)
                remote(
                    part.at[first_of(s, p) // LANES], terms.at[me], term_send.at[0],
                    term_recv.at[0], (s, p),
                ).start()
    first = first_of(slab, loop)
    terms[me] = part[first // LANES]
    sent = 2 + (2 if relayed else lines - 1) + 2 * (lines - 1) + (loops - 3) * lines + loops * lines
    settle(docs.at[pl.ds(0, sent * share)], cand_send.at[0])
    if relayed:
        @pl.when(jnp.logical_not(edge))
        def _():
            settle(docs.at[pl.ds(0, 2 * share)], relay_send.at[0])
    settle(req_in.at[pl.ds(0, slabs - 1)], req_send.at[0])
    settle(picked.at[:, pl.ds(0, slabs - 1)], pick_send.at[0])
    settle(terms.at[pl.ds(0, units - 1)], term_recv.at[0])
    settle(terms.at[pl.ds(0, units - 1)], term_send.at[0])
    row = jnp.sum(terms[...], axis=0)
    mine = lax.broadcasted_iota(jnp.int32, (LANES, LANES), 0)
    to = lax.broadcasted_iota(jnp.int32, (LANES, LANES), 1)
    column_of = jnp.sum(
        jnp.where(mine == to, jnp.broadcast_to(row, (LANES, LANES)), 0.0), axis=1, keepdims=True
    )
    moved = jnp.sum(
        jnp.where(mine == to + lax.rem(first, LANES), column_of, 0.0), axis=0, keepdims=True
    )
    out_ref[...] = moved[:, :share]


def body(dims, doc_pool, cand_owner, cand_row, elements, coverage, elem_weight):
    slabs, loops, share, cap, chunks, chunk, tile, _, _ = dims
    pool_rows, width = doc_pool.shape[2:]
    n_docs = elements.shape[2]
    units = slabs * loops
    vmem = pl.BlockSpec(memory_space=pltpu.VMEM)
    hbm = pl.BlockSpec(memory_space=pl.ANY)
    dma = pltpu.SemaphoreType.DMA
    out = pl.pallas_call(
        functools.partial(kernel, dims),
        out_shape=jax.ShapeDtypeStruct((1, share), jnp.float32),
        in_specs=[vmem, vmem, vmem, vmem, hbm, hbm],
        out_specs=vmem,
        scratch_shapes=[
            pltpu.VMEM((pool_rows, width), jnp.bfloat16),
            pltpu.VMEM((n_docs, width), jnp.bfloat16),
            pltpu.VMEM((slabs, SUB, LANES), jnp.int32),
            pltpu.VMEM((slabs, SUB, LANES), jnp.int32),
            pltpu.VMEM((chunks, slabs, cap, chunk), jnp.bfloat16),
            pltpu.VMEM((chunks, slabs, cap, chunk), jnp.bfloat16),
            pltpu.VMEM((chunks, 2, loops, slabs // 2, share, chunk), jnp.bfloat16),
            pltpu.VMEM((n_docs, units * share), jnp.float32),
            pltpu.VMEM((units * share // LANES, 1, LANES), jnp.float32),
            pltpu.VMEM((units, 1, LANES), jnp.float32),
            dma((1,)),
            dma((1,)),
            dma((1,)),
            dma((1,)),
            dma((1,)),
            dma((chunks,)),
            dma((1,)),
            dma((1,)),
            dma((chunks,)),
            dma((chunks, loops - 1)),
            dma((chunks,)),
            dma((1,)),
            dma((1,)),
        ],
        compiler_params=pltpu.CompilerParams(
            collective_id=0, has_side_effects=True, vmem_limit_bytes=60 * 2**20
        ),
    )(
        cand_owner.reshape(1, share),
        cand_row.reshape(1, share),
        coverage.reshape(n_docs // LANES, LANES),
        elem_weight.reshape(n_docs // LANES, LANES),
        doc_pool.reshape(pool_rows, width),
        elements.reshape(n_docs, width),
    )
    return out.reshape(1, 1, share)


def solution(mesh):
    slabs, loops = mesh.shape["slab"], mesh.shape["loop"]

    def whole(doc_pool, cand_owner, cand_row, elements, coverage, elem_weight):
        share = cand_row.shape[2]
        width = doc_pool.shape[3]
        n_docs = elements.shape[2]
        cap = max(2, 2 * share // slabs)
        dims = (
            slabs, loops, share, cap, CHUNKS, width // CHUNKS, min(512, n_docs),
            float(n_docs * slabs * loops), float(width) ** (-0.5),
        )
        placed = (
            P("slab", "loop", None, None),
            P("slab", "loop", None, None),
            P("slab", "loop", None),
            P("slab", "loop", None, None),
            P("slab", "loop", None),
            P("slab", "loop", None),
        )
        return jax.shard_map(
            functools.partial(body, dims), mesh=mesh, in_specs=placed,
            out_specs=P("slab", "loop", None), check_vma=False,
        )(doc_pool, cand_owner, cand_row, elements, coverage, elem_weight)

    return whole
```

time: 58.4 us -> 50.2 us (0.86)
  Pallas kernels: 57 us -> 48.8 us
    pallas_call x1, Pallas kernels: 57 us -> 48.8 us  [body(): pl.pallas_call(functools.partial(kernel, dims), out_shape=jax.ShapeDtypeS...]
where the time goes in v1:
time: 50.2 us; the launch traced here: 50 us
  Pallas kernels  48.8 us (97%)
  local copies, waits for them, and re-layouts  1.19 us (2%)
    pallas_call x1, Pallas kernels, body(): pl.pallas_call(functools.partial(kernel, dims), out_shape=jax.ShapeDtypeS...  48.8 us
    unnamed x1, local copies, waits for them, and re-layouts  1.19 us

profile of v1, /device:TPU:0, one launch (start us, length us, event | category | flops | bytes accessed | tf_op | source)
XLA Modules:
  0.0 50.0 jit_solution(5726732351860821609)
XLA Ops:
  0.0 48.8 %shard_map.64 = f32[1,16]{1,0:T(1,128)} custom-call(s32[1,16]{1,0:T(1,128)} %bitcast.11, s32[1,16]{1,0:T(1,128)} %bitcast.12, f32[16,128]{1,0:T(8,128)} %bitcast.9, f32[16,128]{1,0:T(8,128)} %bitcast.10, bf16[256,4096]{1,0:T(8,128)(2,1)} %bitcast.8, bf16[2048,4096]{1,0:T(8,128)(2,1)} %bitcast.7), custom_call_target="tpu_custom_call" | custom-call | tf_op jit(solution)/shard_map/pallas_call | solution.py:314
  48.8 1.2 %copy.8 = f32[1,1,16]{2,1,0:T(1,128)} copy(f32[1,1,16]{2,1,0:T(1,128)} %bitcast.13) | data formatting | bytes 128

commit v2 on v1

--- a/solution.py
+++ b/solution.py
@@ -11,7 +11,8 @@
 LANES = 128
 SUB = 8
 CHUNKS = 8
-RING_LAG = 2
+OWN_LEAD = 4
+RING_LAG = 3
 HOP_LAG = 2
 LAST_LAG = 1
 
@@ -242,18 +243,20 @@
 
     for k in range(chunks):
         gather(k)
-    for k in range(chunks):
+    for k in range(min(OWN_LEAD, chunks)):
         own(k)
     lags = [RING_LAG + HOP_LAG * (e - 1) for e in range(1, half + 1)]
     final = lags[-1] + LAST_LAG
     total = jnp.zeros((1, units * share), jnp.float32)
     for t in range(chunks + final):
         stages = []
-        if t < chunks:
-            stages.append(functools.partial(column, t))
+        if t + OWN_LEAD < chunks:
+            stages.append(functools.partial(own, t + OWN_LEAD))
         for e in range(1, half + 1):
             if 0 <= t - lags[e - 1] < chunks:
                 stages.append(functools.partial(ring, t - lags[e - 1], e))
+        if t < chunks:
+            stages.append(functools.partial(column, t))
         done = t - final
         if done >= 0:
             settle(cand.at[done, 0], pair_recv.at[done])

time: 50.2 us -> 49.4 us (0.984)
  Pallas kernels: 48.8 us -> 48 us
    pallas_call x1, Pallas kernels: 48.8 us -> 48 us  [body(): pl.pallas_call(functools.partial(kernel, dims), out_shape=jax.ShapeDtypeS...]
where the time goes in v2:
time: 49.4 us; the launch traced here: 49.2 us
  Pallas kernels  48 us (97%)
  local copies, waits for them, and re-layouts  1.19 us (2%)
    pallas_call x1, Pallas kernels, body(): pl.pallas_call(functools.partial(kernel, dims), out_shape=jax.ShapeDtypeS...  48 us
    unnamed x1, local copies, waits for them, and re-layouts  1.19 us

profile of v2, /device:TPU:0, one launch (start us, length us, event | category | flops | bytes accessed | tf_op | source)
XLA Modules:
  0.0 49.2 jit_solution(6606440998986957076)
XLA Ops:
  0.0 48.0 %shard_map.64 = f32[1,16]{1,0:T(1,128)} custom-call(s32[1,16]{1,0:T(1,128)} %bitcast.11, s32[1,16]{1,0:T(1,128)} %bitcast.12, f32[16,128]{1,0:T(8,128)} %bitcast.9, f32[16,128]{1,0:T(8,128)} %bitcast.10, bf16[256,4096]{1,0:T(8,128)(2,1)} %bitcast.8, bf16[2048,4096]{1,0:T(8,128)(2,1)} %bitcast.7), custom_call_target="tpu_custom_call" | custom-call | tf_op jit(solution)/shard_map/pallas_call | solution.py:317
  48.0 1.2 %copy.8 = f32[1,1,16]{2,1,0:T(1,128)} copy(f32[1,1,16]{2,1,0:T(1,128)} %bitcast.13) | data formatting | bytes 128
